TPU v7x, 32 devices: a whole 2x2x4 slice. The times are simulated.
32 devices in a mesh: leaf: 4 (over z), inner: 8 (over y, x, core).
Axes of the slice: x: 2, y: 2, z: 4, core: 2. Of those that a mesh axis runs over, the one named last changes fastest.
Arguments:
- sources: bfloat16 [16384, 640], P(('leaf', 'inner')), may hold values from -6 to 6
- leaf_perm: int32 [32, 512], P(('leaf', 'inner')), may hold values from 0 to 511, each once within a row
- leaf_factor: bfloat16 [16384, 512], P(('leaf', 'inner')), may hold values from -0.25 to 0.25
- owner_map: int32 [2, 4096], P(None, 'inner'), may hold values from 0 to 1
- coupling: float32 [2, 16384], P(None, ('leaf', 'inner')), may hold values from -0.8 to 0.8
- transfer: bfloat16 [3, 2, 16384, 512], P(None, None, ('leaf', 'inner')), may hold values from -0.1875 to 0.1875
Outputs:
- targets: bfloat16 [16384, 640], P(('leaf', 'inner'))
Inputs may be any that keep to these rules, and one draw needn't show every extreme that they name: Each row of leaf_perm names every number of 0 to 511 once.
All inputs are finite; a program needn't handle non-finite values.
Results may differ from a plain program's by a relative error of at most 0.007.
Values may be sent and summed in bfloat16 or wider, within the bound.
A program may use at most 64 MiB of HBM per device.

v0:
```python
import jax
import jax.numpy as jnp
from jax import lax
from jax.sharding import PartitionSpec as P


def from_partner(value, axis, bit):
    return lax.ppermute(value, axis, [(i, i ^ 1 << bit) for i in range(lax.axis_size(axis))])


def complex_apply(weights, columns):
    real_part = jnp.dot(weights[0], columns, preferred_element_type=jnp.float32)
    imag_part = jnp.dot(weights[1], columns, preferred_element_type=jnp.float32)
    column_half = columns.shape[1] // 2
    return jnp.concatenate(
        [
            real_part[:, :column_half] - imag_part[:, column_half:],
            real_part[:, column_half:] + imag_part[:, :column_half],
        ],
        axis=1,
    )


def precondition(factor, source_rows):
    height = factor.shape[0]
    row_iota = lax.broadcasted_iota(jnp.int32, (height, height), 0)
    col_iota = lax.broadcasted_iota(jnp.int32, (height, height), 1)
    real_lower = jnp.where(row_iota >= col_iota, factor, jnp.zeros_like(factor))
    imag_lower = jnp.where(row_iota > col_iota, factor.T, jnp.zeros_like(factor))
    lower = jnp.stack([real_lower, imag_lower])
    return (source_rows.astype(jnp.float32) + complex_apply(lower, source_rows)).astype(
        jnp.bfloat16
    )


def body(sources, leaf_perm, leaf_factor, owner_map, coupling, transfer):
    height = leaf_factor.shape[0]
    half_rows = height // 2
    column_half = sources.shape[1] // 2
    permuted = jnp.take(sources, leaf_perm[0], axis=0)
    prepared = precondition(leaf_factor, permuted)
    sibling_rows = from_partner(prepared, "leaf", 0)
    leaf_index = lax.axis_index("leaf")
    which_side = leaf_index % 2
    owner_row = lax.dynamic_slice_in_dim(owner_map, leaf_index // 2, 1, 0)[0]
    own_first = (owner_row == which_side)[:, None]
    first_part = jnp.where(own_first, prepared, sibling_rows).astype(jnp.float32)
    other_part = jnp.where(own_first, sibling_rows, prepared).astype(jnp.float32)
    couple_real = coupling[0][:, None]
    couple_imag = coupling[1][:, None]
    mixed_real = (
        first_part[:, :column_half]
        + couple_real * other_part[:, :column_half]
        - couple_imag * other_part[:, column_half:]
    )
    mixed_imag = (
        first_part[:, column_half:]
        + couple_real * other_part[:, column_half:]
        + couple_imag * other_part[:, :column_half]
    )
    field_now = jnp.concatenate([mixed_real, mixed_imag], axis=1).astype(jnp.bfloat16)
    log_size = lax.axis_size("inner").bit_length() - 1
    inner_index = lax.axis_index("inner")
    for section_number in range(transfer.shape[0]):
        bit_number = log_size - 1 - section_number
        which_half = inner_index >> bit_number & 1
        kept_start = which_half * half_rows
        other_start = (1 - which_half) * half_rows
        own_rows = lax.dynamic_slice_in_dim(field_now, kept_start, half_rows, 0)
        outgoing = lax.dynamic_slice_in_dim(field_now, other_start, half_rows, 0)
        partner_rows = from_partner(outgoing, "inner", bit_number)
        weights = transfer[section_number]
        own_cols = lax.dynamic_slice_in_dim(weights, kept_start, half_rows, 2)
        partner_cols = lax.dynamic_slice_in_dim(weights, other_start, half_rows, 2)
        field_now = (
            complex_apply(own_cols, own_rows) + complex_apply(partner_cols, partner_rows)
        ).astype(jnp.bfloat16)
    return field_now


def solution(mesh):
    placed = (
        P(("leaf", "inner"), None),
        P(("leaf", "inner"), None),
        P(("leaf", "inner"), None),
        P(None, "inner"),
        P(None, ("leaf", "inner")),
        P(None, None, ("leaf", "inner"), None),
    )
    return jax.shard_map(
        body, mesh=mesh, in_specs=placed, out_specs=P(("leaf", "inner"), None), check_vma=False
    )
```

profile of v0, /device:TPU:0, one launch (start us, length us, event | category | flops | bytes accessed | tf_op | source)
XLA Modules:
  0.0 50.8 jit_solution(3969071296199575464)
XLA Ops:
  0.0 0.0 copy-start
  0.0 0.8 %compare_select_fusion = s32[512,1]{0,1:T(1,128)S(1)} fusion(s32[1,512]{1,0:T(1,128)} %param.7), kind=kLoop, calls=%fused_computation.75 | loop fusion | flops 1536 | bytes 4096 | tf_op jit(solution)/shard_map/jit(_take)/jit(_where)/select_n | solution.py:40
  0.8 0.7 %compare_and_fusion = pred[512]{0:T(512)(128)(4,1)S(1)} fusion(s32[512]{0:T(512)} %bitcast.56), kind=kLoop, calls=%fused_computation.94 | loop fusion | flops 3072 | bytes 2560 | tf_op jit(solution)/shard_map/jit(_take)/and | solution.py:40
  1.5 1.3 %copy.8 = bf16[512,512]{0,1:T(8,128)(2,1)S(1)} copy(bf16[512,512]{1,0:T(8,128)(2,1)} %param.8) | data formatting | bytes 1048576 | tf_op args[2]
  2.7 0.0 copy-done
  2.7 0.0 copy-start.1
  2.7 2.0 %gather_fusion = bf16[512,640]{1,0:T(8,128)(2,1)S(1)} fusion(bf16[512,640]{1,0:T(8,128)(2,1)S(1)} %copy-done, s32[1024]{0:T(1024)S(1)} %pad_clamp_fusion), kind=kCustom, calls=%fused_computation | custom fusion | bytes 1312768 | tf_op jit(solution)/shard_map/jit(_take)/gather | solution.py:40
  4.8 0.0 copy-done.1
  4.8 0.7 %fusion.10 = f32[512,640]{1,0:T(8,128)S(1)} fusion(bf16[512,512]{1,0:T(8,128)(2,1)S(1)} %copy-done.1, bf16[512,640]{1,0:T(8,128)(2,1)S(1)} %gather_fusion, pred[512]{0:T(512)(128)(4,1)S(1)} %compare_and_fusion), kind=kOutput, calls=%fused_computation.40 | convolution fusion | flops 336396288 | bytes 2490880 | tf_op jit(solution)/shard_map/dot_general | solution.py:13
  5.4 0.7 %fusion.12 = f32[512,640]{1,0:T(8,128)S(1)} fusion(bf16[512,512]{0,1:T(8,128)(2,1)S(1)} %copy.8, bf16[512,640]{1,0:T(8,128)(2,1)S(1)} %gather_fusion, pred[512]{0:T(512)(128)(4,1)S(1)} %compare_and_fusion), kind=kOutput, calls=%fused_computation.41 | convolution fusion | flops 336396288 | bytes 2490880 | tf_op jit(solution)/shard_map/dot_general | solution.py:12
  6.1 0.5 slice_subtract_fusion.6
  6.6 0.0 copy-start.3
  6.6 0.0 copy-start.2
  6.6 0.5 fusion
  7.1 3.1 %collective-permute-start = (bf16[512,640]{1,0:T(8,128)(2,1)S(1)}, bf16[512,640]{1,0:T(8,128)(2,1)S(1)}, u32[]{:S(2)}, u32[]{:S(2)}) collective-permute-start(bf16[512,640]{1,0:T(8,128)(2,1)S(1)} %fusion), channel_id=1, source_target_pairs={{0,8},{8,0},{16,24},{24,16},{1,9},{9,1},{17,25},{25,17},{2,10},{10... | collective-permute-start | bytes 1966088 | tf_op jit(solution)/shard_map/ppermute | solution.py:8
  10.2 0.0 copy-done.3
  10.2 0.0 copy-done.2
  10.2 2.1 %fusion.51 = (bf16[1,2,512,512]{3,2,1,0:T(8,128)(2,1)S(1)}, bf16[1,2,512,512]{3,2,1,0:T(8,128)(2,1)S(1)}, bf16[1,2,512,512]{3,2,1,0:T(8,128)(2,1)S(1)}) fusion(bf16[3,2,512,512]{3,2,1,0:T(8,128)(2,1)} %param.11), kind=kLoop, calls=%fused_computation.97 | loop fusion | bytes 6291456 | tf_op jit(solution)/shard_map/slice | solution.py:72
  12.3 12.6 %collective-permute-done = bf16[512,640]{1,0:T(8,128)(2,1)S(1)} collective-permute-done((bf16[512,640]{1,0:T(8,128)(2,1)S(1)}, bf16[512,640]{1,0:T(8,128)(2,1)S(1)}, u32[]{:S(2)}, u32[]{:S(2)}) %collective-permute-start) | collective-permute-done | bytes 655392 | tf_op jit(solution)/shard_map/ppermute | solution.py:8
  24.9 0.2 select_convert_fusion
  25.2 0.7 %fusion.7 = (bf16[512,320]{1,0:T(8,128)(2,1)S(1)}, bf16[512,320]{1,0:T(8,128)(2,1)S(1)}) fusion(f32[512,640]{1,0:T(8,128)S(1)} %get-tuple-element.25, f32[512,640]{1,0:T(8,128)S(1)} %get-tuple-element.24, f32[512]{0:T(512)S(1)} %bitcast.54, f32[512]{0:T(512)S(1)} %bitcast.53), kind=kLoop, calls=%fused_computation.27 | loop fusion | flops 1638400 | bytes 3280896 | tf_op jit(solution)/shard_map/convert.1
  25.9 0.1 fusion.15
  26.0 1.7 %collective-permute-start.1 = (bf16[256,640]{1,0:T(8,128)(2,1)S(1)}, bf16[256,640]{1,0:T(8,128)(2,1)S(1)}, u32[]{:S(2)}, u32[]{:S(2)}) collective-permute-start(bf16[256,640]{1,0:T(8,128)(2,1)S(1)} %fusion.15), channel_id=1, source_target_pairs={{0,4},{1,5},{2,6},{3,7},{4,0},{5,1},{6,2},{7,3},{8,12},{9,13},{10,... | collective-permute-start | bytes 983048 | tf_op jit(solution)/shard_map/ppermute | solution.py:8
  27.8 0.4 fusion.32
  28.2 0.4 fusion.31
  28.6 0.5 slice_subtract_fusion.5
  29.1 5.9 %collective-permute-done.1 = bf16[256,640]{1,0:T(8,128)(2,1)S(1)} collective-permute-done((bf16[256,640]{1,0:T(8,128)(2,1)S(1)}, bf16[256,640]{1,0:T(8,128)(2,1)S(1)}, u32[]{:S(2)}, u32[]{:S(2)}) %collective-permute-start.1) | collective-permute-done | bytes 327712 | tf_op jit(solution)/shard_map/ppermute | solution.py:8
  35.0 0.4 fusion.30
  35.3 0.4 fusion.29
  35.7 0.5 slice_subtract_fusion.4
  36.2 0.5 fusion.1
  36.7 1.4 %collective-permute-start.2 = (bf16[256,640]{1,0:T(8,128)(2,1)S(1)}, bf16[256,640]{1,0:T(8,128)(2,1)S(1)}, u32[]{:S(2)}, u32[]{:S(2)}) collective-permute-start(bf16[256,640]{1,0:T(8,128)(2,1)S(1)} %constant_dynamic-slice_fusion.1), channel_id=1, source_target_pairs={{0,2},{1,3},{2,0},{3,1},{4,6},{5,7},{6,4},{7,5},{8,10},{9,11},{10,... | collective-permute-start | bytes 983048 | tf_op jit(solution)/shard_map/ppermute | solution.py:8
  38.2 0.4 fusion.23
  38.5 0.4 fusion.21
  38.9 0.5 slice_subtract_fusion.3
  39.4 5.4 %collective-permute-done.2 = bf16[256,640]{1,0:T(8,128)(2,1)S(1)} collective-permute-done((bf16[256,640]{1,0:T(8,128)(2,1)S(1)}, bf16[256,640]{1,0:T(8,128)(2,1)S(1)}, u32[]{:S(2)}, u32[]{:S(2)}) %collective-permute-start.2) | collective-permute-done | bytes 327712 | tf_op jit(solution)/shard_map/ppermute | solution.py:8
  44.8 0.4 fusion.27
  45.2 0.4 fusion.28
  45.6 0.5 slice_subtract_fusion.2
  46.0 0.5 fusion.2
  46.6 0.1 collective-permute-start.3
  46.6 0.4 fusion.19
  47.0 0.4 fusion.17
  47.4 0.5 slice_subtract_fusion.1
  47.9 0.4 collective-permute-done.3
  48.3 0.4 fusion.25
  48.6 0.4 fusion.26
  49.0 0.5 slice_subtract_fusion
  49.5 1.3 %fusion.3 = bf16[512,640]{1,0:T(8,128)(2,1)} fusion(f32[512,320]{1,0:T(8,128)S(1)} %get-tuple-element.13, f32[512,320]{1,0:T(8,128)S(1)} %get-tuple-element.12, f32[512,320]{1,0:T(8,128)S(1)} %get-tuple-element.11, f32[512,320]{1,0:T(8,128)S(1)} %get-tuple-element.10), kind=kLoop, calls=%fused_computation.8 | loop fusion | flops 1310720 | bytes 3276800 | tf_op jit(solution)/shard_map/convert_element_type | solution.py:77
  (5 shorter events, 0.1 us)
Async XLA Ops:
  0.0 2.7 %copy-start = (bf16[512,640]{1,0:T(8,128)(2,1)S(1)}, bf16[512,640]{1,0:T(8,128)(2,1)}, u32[]{:S(2)}) copy-start(bf16[512,640]{1,0:T(8,128)(2,1)} %param.6) | copy-start | bytes 1966084
  2.7 2.0 %copy-start.1 = (bf16[512,512]{1,0:T(8,128)(2,1)S(1)}, bf16[512,512]{1,0:T(8,128)(2,1)}, u32[]{:S(2)}) copy-start(bf16[512,512]{1,0:T(8,128)(2,1)} %param.8) | copy-start | bytes 1572868
  6.6 3.6 %copy-start.3 = (s32[2,512]{1,0:T(2,128)S(1)}, s32[2,512]{1,0:T(2,128)}, u32[]{:S(2)}) copy-start(s32[2,512]{1,0:T(2,128)} %param.9) | copy-start | bytes 12292
  6.6 3.6 %copy-start.2 = (f32[2,512]{1,0:T(2,128)S(1)}, f32[2,512]{1,0:T(2,128)}, u32[]{:S(2)}) copy-start(f32[2,512]{1,0:T(2,128)} %param.10) | copy-start | bytes 12292
  7.1 17.9 %collective-permute-start = (bf16[512,640]{1,0:T(8,128)(2,1)S(1)}, bf16[512,640]{1,0:T(8,128)(2,1)S(1)}, u32[]{:S(2)}, u32[]{:S(2)}) collective-permute-start(bf16[512,640]{1,0:T(8,128)(2,1)S(1)} %fusion), channel_id=1, source_target_pairs={{0,8},{8,0},{16,24},{24,16},{1,9},{9,1},{17,25},{25,17},{2,10},{10... | collective-permute-start | bytes 1966088 | tf_op jit(solution)/shard_map/ppermute | solution.py:8
  26.0 8.9 %collective-permute-start.1 = (bf16[256,640]{1,0:T(8,128)(2,1)S(1)}, bf16[256,640]{1,0:T(8,128)(2,1)S(1)}, u32[]{:S(2)}, u32[]{:S(2)}) collective-permute-start(bf16[256,640]{1,0:T(8,128)(2,1)S(1)} %fusion.15), channel_id=1, source_target_pairs={{0,4},{1,5},{2,6},{3,7},{4,0},{5,1},{6,2},{7,3},{8,12},{9,13},{10,... | collective-permute-start | bytes 983048 | tf_op jit(solution)/shard_map/ppermute | solution.py:8
  36.7 8.1 %collective-permute-start.2 = (bf16[256,640]{1,0:T(8,128)(2,1)S(1)}, bf16[256,640]{1,0:T(8,128)(2,1)S(1)}, u32[]{:S(2)}, u32[]{:S(2)}) collective-permute-start(bf16[256,640]{1,0:T(8,128)(2,1)S(1)} %constant_dynamic-slice_fusion.1), channel_id=1, source_target_pairs={{0,2},{1,3},{2,0},{3,1},{4,6},{5,7},{6,4},{7,5},{8,10},{9,11},{10,... | collective-permute-start | bytes 983048 | tf_op jit(solution)/shard_map/ppermute | solution.py:8
  46.6 1.7 %collective-permute-start.3 = (bf16[256,640]{1,0:T(8,128)(2,1)S(1)}, bf16[256,640]{1,0:T(8,128)(2,1)S(1)}, u32[]{:S(2)}, u32[]{:S(2)}) collective-permute-start(bf16[256,640]{1,0:T(8,128)(2,1)S(1)} %constant_dynamic-slice_fusion), channel_id=1, source_target_pairs={{0,1},{1,0},{2,3},{3,2},{4,5},{5,4},{6,7},{7,6},{8,9},{9,8},{10,11... | collective-permute-start | bytes 983048 | tf_op jit(solution)/shard_map/ppermute | solution.py:8
where the time goes:
time: 51 us; the launch traced here: 50.8 us
  waiting for transfers between devices  24.3 us (48%)
  other arithmetic  8.63 us (17%)
  starting transfers between devices  6.38 us (13%)
  matrix products  5.88 us (12%)
  local copies, waits for them, and re-layouts  5.45 us (11%)
    ppermute x4, waiting for transfers between devices, from_partner(): lax.ppermute(value, axis, [(i, i ^ 1 << bit) for i in range(lax.axis_size...  24.3 us
    ppermute x4, starting transfers between devices, from_partner(): lax.ppermute(value, axis, [(i, i ^ 1 << bit) for i in range(lax.axis_size...  6.38 us
    sub x7, other arithmetic, complex_apply(): real_part[:, :column_half] - imag_part[:, column_half:]  3.31 us
    dot_general x7, matrix products, complex_apply(): imag_part = jnp.dot(weights[1], columns, preferred_element_type=jnp.float32)  2.94 us
    dot_general x7, matrix products, complex_apply(): real_part = jnp.dot(weights[0], columns, preferred_element_type=jnp.float32)  2.94 us
    convert_element_type x3, other arithmetic, body(): field_now = (complex_apply(own_cols, own_rows) + complex_apply(partner_co...  2.29 us
    slice x1, local copies, waits for them, and re-layouts, body(): weights = transfer[section_number]  2.06 us
    gather x1, local copies, waits for them, and re-layouts, body(): permuted = jnp.take(sources, leaf_perm[0], axis=0)  2.02 us
  transfers between devices with their start and end apart: 4, of which 4 were waited for; matrix products, arithmetic and copies ran while one was open for 12% of the time, Pallas kernels for 0%

commit v1 on v0

v1 whole, which is shorter than its diff:
```python
import functools

import jax
import jax.numpy as jnp
from jax import lax
from jax.experimental import pallas as pl
from jax.experimental.pallas import tpu as pltpu
from jax.sharding import PartitionSpec as P

LANES = 128
PIECE = LANES // 2
MESH = pl.DeviceIdType.MESH
F32 = jnp.float32
BF16 = jnp.bfloat16


def dot(a, b):
    return jnp.dot(a, b, preferred_element_type=F32)


def as_column(row):
    return jnp.broadcast_to(row, (LANES, row.shape[1])).T


def kernel(
    levels,
    perm_ref,
    owner_ref,
    couple_ref,
    source_hbm,
    factor_hbm,
    transfer_hbm,
    out_ref,
    source,
    factor,
    weights,
    lower_real,
    lower_imag,
    mine,
    prepared,
    theirs,
    inputs,
    outgoing,
    final,
    partner_couple,
    partner_owner,
    load_sem,
    small_send,
    small_recv,
    side_send,
    side_recv,
    sib_send,
    sib_recv,
    level_send,
    level_recv,
):
    height, width = source.shape
    half = height // 2
    pieces = width // LANES
    leaf = lax.axis_index("leaf")
    inner = lax.axis_index("inner")
    inner_size = lax.axis_size("inner")
    sibling = leaf + 1 - 2 * lax.rem(leaf, 2)
    which_side = lax.rem(leaf, 2)
    pair = leaf // 2

    bits, partners = [], []
    for level in range(levels):
        distance = inner_size >> (level + 1)
        bit = lax.rem(inner // distance, 2)
        bits.append(bit)
        partners.append(inner + distance - 2 * distance * bit)

    def rows_at(flag):
        return pl.ds(pl.multiple_of(flag * half, half), half)

    loads = [
        pltpu.make_async_copy(source_hbm, source, load_sem.at[0]),
        pltpu.make_async_copy(factor_hbm, factor, load_sem.at[1]),
    ]
    for level in range(levels):
        loads.append(
            pltpu.make_async_copy(
                transfer_hbm.at[level], weights.at[level], load_sem.at[2 + level]
            )
        )
    for load in loads:
        load.start()

    barrier = pltpu.get_barrier_semaphore()
    pl.semaphore_signal(barrier, inc=1, device_id={"leaf": sibling}, device_id_type=MESH)
    for level in range(levels):
        pl.semaphore_signal(
            barrier, inc=1, device_id={"inner": partners[level]}, device_id_type=MESH
        )

    lane = lax.broadcasted_iota(jnp.int32, (height, LANES), 1)
    low_lanes = lane < PIECE
    sign_even = jnp.where(low_lanes, -1.0, 1.0).astype(F32)

    def turned(value, piece):
        rolled = pltpu.roll(value, PIECE, 1)
        sign = sign_even[: value.shape[0]]
        return rolled * sign if piece % 2 == 0 else rolled * -sign

    perm_column = as_column(perm_ref[...])
    one_hot = jnp.concatenate(
        [
            jnp.where(perm_column == lane + LANES * tile, 1.0, 0.0).astype(BF16)
            for tile in range(height // LANES)
        ],
        axis=1,
    )

    loads[1].wait()
    row_half = lax.broadcasted_iota(jnp.int32, (half, half), 0)
    col_half = lax.broadcasted_iota(jnp.int32, (half, half), 1)
    for part in range(2):
        here = slice(part * half, (part + 1) * half)
        block = factor[here, here].astype(F32)
        lower_real[here, here] = jnp.where(row_half >= col_half, block, 0.0).astype(BF16)
        lower_imag[here, here] = jnp.where(row_half > col_half, block.T, 0.0).astype(BF16)
    lower_real[half:, :half] = factor[half:, :half]
    lower_imag[half:, :half] = factor[:half, half:].astype(F32).T.astype(BF16)

    loads[0].wait()
    pl.semaphore_wait(barrier, levels + 1)

    small = [
        pltpu.make_async_remote_copy(
            src_ref=couple_ref,
            dst_ref=partner_couple,
            send_sem=small_send.at[0],
            recv_sem=small_recv.at[0],
            device_id={"inner": partners[0]},
            device_id_type=MESH,
        ),
        pltpu.make_async_remote_copy(
            src_ref=owner_ref,
            dst_ref=partner_owner,
            send_sem=small_send.at[1],
            recv_sem=small_recv.at[1],
            device_id={"inner": partners[0]},
            device_id_type=MESH,
        ),
    ]
    for copy in small:
        copy.start()

    kept, other = rows_at(bits[0]), rows_at(1 - bits[0])

    def side_copy(piece):
        return pltpu.make_async_remote_copy(
            src_ref=mine.at[piece],
            dst_ref=prepared.at[piece, kept],
            send_sem=side_send.at[piece],
            recv_sem=side_recv.at[piece],
            device_id={"inner": partners[0]},
            device_id_type=MESH,
        )

    def sibling_copy(piece, stage):
        rows = kept if stage == 0 else other
        return pltpu.make_async_remote_copy(
            src_ref=prepared.at[piece, rows],
            dst_ref=theirs.at[piece, rows],
            send_sem=sib_send.at[stage, piece],
            recv_sem=sib_recv.at[stage, piece],
            device_id={"leaf": sibling},
            device_id_type=MESH,
        )

    def level_copy(level, piece):
        return pltpu.make_async_remote_copy(
            src_ref=outgoing.at[level - 1, piece],
            dst_ref=inputs.at[level, piece, rows_at(bits[level])],
            send_sem=level_send.at[level - 1, piece],
            recv_sem=level_recv.at[level - 1, piece],
            device_id={"inner": partners[level]},
            device_id_type=MESH,
        )

    def prepare(piece):
        real_tile, imag_tile = piece // 2, (pieces + piece) // 2
        low_tile, high_tile = (
            (real_tile, imag_tile) if piece % 2 == 0 else (imag_tile, real_tile)
        )
        column = jnp.where(
            low_lanes,
            source[:, low_tile * LANES : (low_tile + 1) * LANES].astype(F32),
            source[:, high_tile * LANES : (high_tile + 1) * LANES].astype(F32),
        ).astype(BF16)
        permuted = dot(one_hot, column)
        permuted_half = permuted.astype(BF16)
        results = []
        for part in range(2):
            here = slice(part * half, (part + 1) * half)
            depth = (part + 1) * half
            real_part = dot(lower_real[here, :depth], permuted_half[:depth])
            imag_part = dot(lower_imag[here, :depth], permuted_half[:depth])
            results.append(
                (permuted[here] + real_part + turned(imag_part, piece)).astype(BF16)
            )
        top, bottom = results
        upper = bits[0] == 1
        prepared[piece, kept, :] = jnp.where(upper, bottom, top)
        mine[piece] = jnp.where(upper, top, bottom)
        sibling_copy(piece, 0).start()
        side_copy(piece).start()

    def forward(piece):
        side_copy(piece).wait_recv()
        sibling_copy(piece, 1).start()

    lag = 2
    for piece in range(pieces):
        prepare(piece)
        if piece >= lag:
            forward(piece - lag)

    for copy in small:
        copy.wait_recv()

    def in_input_order(own, partner):
        low, high = slice(0, half), slice(half, height)
        return jnp.concatenate(
            [
                jnp.where(bits[0] == 0, own[:, low], partner[:, high]),
                jnp.where(bits[0] == 1, own[:, high], partner[:, low]),
            ],
            axis=1,
        )

    couple_rows = in_input_order(couple_ref[...], partner_couple[...])
    owner_rows = in_input_order(
        owner_ref[pl.ds(pair, 1), :], partner_owner[pl.ds(pair, 1), :]
    )
    couple_real = as_column(couple_rows[0:1])
    couple_imag = as_column(couple_rows[1:2])
    own_first = as_column(owner_rows) == which_side

    for piece in range(pieces - lag, pieces):
        forward(piece)

    def combine(piece):
        sibling_copy(piece, 0).wait_recv()
        sibling_copy(piece, 1).wait_recv()
        here = prepared[piece].astype(F32)
        there = theirs[piece].astype(F32)
        first_part = jnp.where(own_first, here, there)
        other_part = jnp.where(own_first, there, here)
        return (
            first_part + couple_real * other_part + couple_imag * turned(other_part, piece)
        ).astype(BF16)

    def rows_of(level, piece, rows, field):
        real_part = dot(weights[level, 0, rows, :], field)
        imag_part = dot(weights[level, 1, rows, :], field)
        return (real_part + turned(imag_part, piece)).astype(BF16)

    loaded = set()

    def run_level(level, piece):
        if level == 0:
            field = combine(piece)
        else:
            level_copy(level, piece).wait_recv()
            field = inputs[level, piece]
        if level not in loaded:
            loads[2 + level].wait()
            loaded.add(level)
        if level + 1 < levels:
            bit = bits[level + 1]
            outgoing[level, piece] = rows_of(level, piece, rows_at(1 - bit), field)
            level_copy(level + 1, piece).start()
            inputs[level + 1, piece, rows_at(bit), :] = rows_of(
                level, piece, rows_at(bit), field
            )
        else:
            final[piece] = rows_of(level, piece, slice(None), field)

    for step in range(pieces + levels - 1):
        for level in range(levels):
            piece = step - level
            if 0 <= piece < pieces:
                run_level(level, piece)

    for tile in range(pieces):
        low_piece, high_piece = [
            place if place < pieces else place - pieces for place in (2 * tile, 2 * tile + 1)
        ]
        out_ref[:, tile * LANES : (tile + 1) * LANES] = jnp.where(
            low_lanes, final[low_piece].astype(F32), final[high_piece].astype(F32)
        ).astype(BF16)

    for copy in small:
        copy.wait_send()
    for piece in range(pieces):
        side_copy(piece).wait_send()
        sibling_copy(piece, 0).wait_send()
        sibling_copy(piece, 1).wait_send()
        for level in range(1, levels):
            level_copy(level, piece).wait_send()


def body(sources, leaf_perm, leaf_factor, owner_map, coupling, transfer):
    height, width = sources.shape
    half = height // 2
    levels = transfer.shape[0]
    pieces = width // LANES
    assert width == pieces * LANES and pieces % 2 == 1
    vmem = pl.BlockSpec(memory_space=pltpu.VMEM)
    anywhere = pl.BlockSpec(memory_space=pl.ANY)
    dma = pltpu.SemaphoreType.DMA
    return pl.pallas_call(
        functools.partial(kernel, levels),
        out_shape=jax.ShapeDtypeStruct(sources.shape, sources.dtype),
        in_specs=[vmem, vmem, vmem, anywhere, anywhere, anywhere],
        out_specs=vmem,
        scratch_shapes=[
            pltpu.VMEM(sources.shape, BF16),
            pltpu.VMEM(leaf_factor.shape, BF16),
            pltpu.VMEM(transfer.shape, BF16),
            pltpu.VMEM(leaf_factor.shape, BF16),
            pltpu.VMEM(leaf_factor.shape, BF16),
            pltpu.VMEM((pieces, half, LANES), BF16),
            pltpu.VMEM((pieces, height, LANES), BF16),
            pltpu.VMEM((pieces, height, LANES), BF16),
            pltpu.VMEM((levels, pieces, height, LANES), BF16),
            pltpu.VMEM((levels - 1, pieces, half, LANES), BF16),
            pltpu.VMEM((pieces, height, LANES), BF16),
            pltpu.VMEM(coupling.shape, coupling.dtype),
            pltpu.VMEM(owner_map.shape, owner_map.dtype),
            dma((2 + levels,)),
            dma((2,)),
            dma((2,)),
            dma((pieces,)),
            dma((pieces,)),
            dma((2, pieces)),
            dma((2, pieces)),
            dma((levels - 1, pieces)),
            dma((levels - 1, pieces)),
        ],
        compiler_params=pltpu.CompilerParams(collective_id=0, has_side_effects=True, vmem_limit_bytes=58 * 1024 * 1024),
        name="apply",
    )(leaf_perm, owner_map, coupling, sources, leaf_factor, transfer)


def solution(mesh):
    placed = (
        P(("leaf", "inner"), None),
        P(("leaf", "inner"), None),
        P(("leaf", "inner"), None),
        P(None, "inner"),
        P(None, ("leaf", "inner")),
        P(None, None, ("leaf", "inner"), None),
    )
    return jax.shard_map(
        body, mesh=mesh, in_specs=placed, out_specs=P(("leaf", "inner"), None), check_vma=False
    )
```

time: 51 us -> 33 us (0.65)
  Pallas kernels: 0 us -> 30.9 us
  waiting for transfers between devices: 24.3 us -> 0 us
  other arithmetic: 8.63 us -> 0 us
  starting transfers between devices: 6.38 us -> 0 us
  matrix products: 5.88 us -> 0 us
  local copies, waits for them, and re-layouts: 5.45 us -> 1.98 us
    pallas_call x0 -> x1, Pallas kernels: none -> 30.9 us  [body(): pl.pallas_call(functools.partial(kernel, levels), out_shape=jax.ShapeDtyp...]
    ppermute x4 -> x0, waiting for transfers between devices: 24.3 us -> none  [from_partner(): lax.ppermute(value, axis, [(i, i ^ 1 << bit) for i in range(lax.axis_size...]
    ppermute x4 -> x0, starting transfers between devices: 6.38 us -> none  [from_partner(): lax.ppermute(value, axis, [(i, i ^ 1 << bit) for i in range(lax.axis_size...]
    dot_general x14 -> x0, matrix products: 5.88 us -> none  [the longest x7 2.94 us: complex_apply(): imag_part = jnp.dot(weights[1], columns, preferred_element_type=jnp.float32)]
    sub x7 -> x0, other arithmetic: 3.31 us -> none  [complex_apply(): real_part[:, :column_half] - imag_part[:, column_half:]]
    convert_element_type x5 -> x0, other arithmetic: 2.98 us -> none  [the longest x3 2.29 us: body(): field_now = (complex_apply(own_cols, own_rows) + complex_apply(partner_co...]
    slice x2 -> x0, local copies, waits for them, and re-layouts: 2.07 us -> none  [the longest x1 2.06 us: body(): weights = transfer[section_number]]
    gather x1 -> x0, local copies, waits for them, and re-layouts: 2.02 us -> none  [body(): permuted = jnp.take(sources, leaf_perm[0], axis=0)]
  transfers between devices with their start and end apart: 4 -> 0, of which waited for: 4 -> 0; matrix products, arithmetic and copies ran while one was open for 12% -> 0% of each run, Pallas kernels for 0% -> 0%
where the time goes in v1:
time: 33 us; the launch traced here: 32.8 us
  Pallas kernels  30.9 us (94%)
  local copies, waits for them, and re-layouts  1.98 us (6%)
    pallas_call x1, Pallas kernels, body(): pl.pallas_call(functools.partial(kernel, levels), out_shape=jax.ShapeDtyp...  30.9 us
    unnamed x1, local copies, waits for them, and re-layouts  1.98 us

profile of v1, /device:TPU:0, one launch (start us, length us, event | category | flops | bytes accessed | tf_op | source)
XLA Modules:
  0.0 32.8 jit_solution(5094763570069877329)
XLA Ops:
  0.0 30.9 %apply.1 = bf16[512,640]{1,0:T(8,128)(2,1)} custom-call(s32[1,512]{1,0:T(1,128)} %perm_ref.1, s32[2,512]{1,0:T(2,128)} %owner_ref.1, f32[2,512]{1,0:T(2,128)} %couple_ref.1, bf16[512,640]{1,0:T(8,128)(2,1)} %source_hbm.1, bf16[512,512]{1,0:T(8,128)(2,1)} %factor_hbm.1, bf16[3,2,512,512]{3,2,1,0:T(8,128)(2,1)} %transfer_hbm.1), custom_call_target="tpu_custom_call" | custom-call | tf_op jit(solution)/shard_map/apply/pallas_call | solution.py:315
  30.9 2.0 %copy.8 = bf16[512,640]{1,0:T(8,128)(2,1)} copy(bf16[512,640]{1,0:T(8,128)(2,1)} %apply.1) | data formatting | bytes 1310720

commit v2 on v1

--- a/solution.py
+++ b/solution.py
@@ -24,13 +24,16 @@
 
 def kernel(
     levels,
-    perm_ref,
-    owner_ref,
-    couple_ref,
+    perm_hbm,
+    owner_hbm,
+    couple_hbm,
     source_hbm,
     factor_hbm,
     transfer_hbm,
     out_ref,
+    perm_ref,
+    owner_ref,
+    couple_ref,
     source,
     factor,
     weights,
@@ -74,19 +77,6 @@
     def rows_at(flag):
         return pl.ds(pl.multiple_of(flag * half, half), half)
 
-    loads = [
-        pltpu.make_async_copy(source_hbm, source, load_sem.at[0]),
-        pltpu.make_async_copy(factor_hbm, factor, load_sem.at[1]),
-    ]
-    for level in range(levels):
-        loads.append(
-            pltpu.make_async_copy(
-                transfer_hbm.at[level], weights.at[level], load_sem.at[2 + level]
-            )
-        )
-    for load in loads:
-        load.start()
-
     barrier = pltpu.get_barrier_semaphore()
     pl.semaphore_signal(barrier, inc=1, device_id={"leaf": sibling}, device_id_type=MESH)
     for level in range(levels):
@@ -94,6 +84,20 @@
             barrier, inc=1, device_id={"inner": partners[level]}, device_id_type=MESH
         )
 
+    load_list = [
+        (perm_hbm, perm_ref),
+        (source_hbm, source),
+        (factor_hbm, factor),
+        (couple_hbm, couple_ref),
+        (owner_hbm, owner_ref),
+    ] + [(transfer_hbm.at[level], weights.at[level]) for level in range(levels)]
+    loads = [
+        pltpu.make_async_copy(origin, place, load_sem.at[number])
+        for number, (origin, place) in enumerate(load_list)
+    ]
+    for load in loads:
+        load.start()
+
     lane = lax.broadcasted_iota(jnp.int32, (height, LANES), 1)
     low_lanes = lane < PIECE
     sign_even = jnp.where(low_lanes, -1.0, 1.0).astype(F32)
@@ -103,6 +107,7 @@
         sign = sign_even[: value.shape[0]]
         return rolled * sign if piece % 2 == 0 else rolled * -sign
 
+    loads[0].wait()
     perm_column = as_column(perm_ref[...])
     one_hot = jnp.concatenate(
         [
@@ -112,7 +117,7 @@
         axis=1,
     )
 
-    loads[1].wait()
+    loads[2].wait()
     row_half = lax.broadcasted_iota(jnp.int32, (half, half), 0)
     col_half = lax.broadcasted_iota(jnp.int32, (half, half), 1)
     for part in range(2):
@@ -123,8 +128,9 @@
     lower_real[half:, :half] = factor[half:, :half]
     lower_imag[half:, :half] = factor[:half, half:].astype(F32).T.astype(BF16)
 
-    loads[0].wait()
-    pl.semaphore_wait(barrier, levels + 1)
+    loads[1].wait()
+    loads[3].wait()
+    loads[4].wait()
 
     small = [
         pltpu.make_async_remote_copy(
@@ -144,9 +150,6 @@
             device_id_type=MESH,
         ),
     ]
-    for copy in small:
-        copy.start()
-
     kept, other = rows_at(bits[0]), rows_at(1 - bits[0])
 
     def side_copy(piece):
@@ -205,8 +208,13 @@
         upper = bits[0] == 1
         prepared[piece, kept, :] = jnp.where(upper, bottom, top)
         mine[piece] = jnp.where(upper, top, bottom)
+        if piece == 0:
+            pl.semaphore_wait(barrier, levels + 1)
         sibling_copy(piece, 0).start()
         side_copy(piece).start()
+        if piece == 0:
+            for copy in small:
+                copy.start()
 
     def forward(piece):
         side_copy(piece).wait_recv()
@@ -267,7 +275,7 @@
             level_copy(level, piece).wait_recv()
             field = inputs[level, piece]
         if level not in loaded:
-            loads[2 + level].wait()
+            loads[5 + level].wait()
             loaded.add(level)
         if level + 1 < levels:
             bit = bits[level + 1]
@@ -315,9 +323,12 @@
     return pl.pallas_call(
         functools.partial(kernel, levels),
         out_shape=jax.ShapeDtypeStruct(sources.shape, sources.dtype),
-        in_specs=[vmem, vmem, vmem, anywhere, anywhere, anywhere],
+        in_specs=[anywhere] * 6,
         out_specs=vmem,
         scratch_shapes=[
+            pltpu.VMEM(leaf_perm.shape, leaf_perm.dtype),
+            pltpu.VMEM(owner_map.shape, owner_map.dtype),
+            pltpu.VMEM(coupling.shape, coupling.dtype),
             pltpu.VMEM(sources.shape, BF16),
             pltpu.VMEM(leaf_factor.shape, BF16),
             pltpu.VMEM(transfer.shape, BF16),
@@ -331,7 +342,7 @@
             pltpu.VMEM((pieces, height, LANES), BF16),
             pltpu.VMEM(coupling.shape, coupling.dtype),
             pltpu.VMEM(owner_map.shape, owner_map.dtype),
-            dma((2 + levels,)),
+            dma((5 + levels,)),
             dma((2,)),
             dma((2,)),
             dma((pieces,)),
@@ -341,9 +352,9 @@
             dma((levels - 1, pieces)),
             dma((levels - 1, pieces)),
         ],
-        compiler_params=pltpu.CompilerParams(collective_id=0, has_side_effects=True, vmem_limit_bytes=58 * 1024 * 1024),
+        compiler_params=pltpu.CompilerParams(collective_id=0, has_side_effects=True, vmem_limit_bytes=20 * 1024 * 1024),
         name="apply",
-    )(leaf_perm, owner_map, coupling, sources, leaf_factor, transfer)
+    )(*[pltpu.with_memory_space_constraint(x, pltpu.HBM) for x in (leaf_perm, owner_map, coupling, sources, leaf_factor, transfer)])
 
 
 def solution(mesh):

time: 33 us -> 30.3 us (0.918)
  Pallas kernels: 30.9 us -> 29.3 us
  local copies, waits for them, and re-layouts: 1.98 us -> 0.84 us
    pallas_call x1, Pallas kernels: 30.9 us -> 29.3 us  [body(): pl.pallas_call(functools.partial(kernel, levels), out_shape=jax.ShapeDtyp...]
    unnamed x1, local copies, waits for them, and re-layouts: 1.98 us -> 0.84 us
where the time goes in v2:
time: 30.3 us; the launch traced here: 30.1 us
  Pallas kernels  29.3 us (97%)
  local copies, waits for them, and re-layouts  0.84 us (3%)
    pallas_call x1, Pallas kernels, body(): pl.pallas_call(functools.partial(kernel, levels), out_shape=jax.ShapeDtyp...  29.3 us
    unnamed x1, local copies, waits for them, and re-layouts  0.84 us

profile of v2, /device:TPU:0, one launch (start us, length us, event | category | flops | bytes accessed | tf_op | source)
XLA Modules:
  0.0 30.1 jit_solution(9374307729799131690)
XLA Ops:
  0.0 29.3 %apply.1 = bf16[512,640]{1,0:T(8,128)(2,1)S(1)} custom-call(s32[1,512]{1,0:T(1,128)} %perm_hbm.1, s32[2,512]{1,0:T(2,128)} %owner_hbm.1, f32[2,512]{1,0:T(2,128)} %couple_hbm.1, bf16[512,640]{1,0:T(8,128)(2,1)} %source_hbm.1, bf16[512,512]{1,0:T(8,128)(2,1)} %factor_hbm.1, bf16[3,2,512,512]{3,2,1,0:T(8,128)(2,1)} %transfer_hbm.1), custom_call_target="tpu_custom_call" | custom-call | tf_op jit(solution)/shard_map/apply/pallas_call | solution.py:323
  29.3 0.8 %copy.8 = bf16[512,640]{1,0:T(8,128)(2,1)} copy(bf16[512,640]{1,0:T(8,128)(2,1)S(1)} %apply.1) | data formatting | bytes 1310720

commit v3 on v2

--- a/solution.py
+++ b/solution.py
@@ -47,6 +47,9 @@
     final,
     partner_couple,
     partner_owner,
+    couple_real_cols,
+    couple_imag_cols,
+    owner_cols,
     load_sem,
     small_send,
     small_recv,
@@ -220,7 +223,7 @@
         side_copy(piece).wait_recv()
         sibling_copy(piece, 1).start()
 
-    lag = 2
+    lag = 5
     for piece in range(pieces):
         prepare(piece)
         if piece >= lag:
@@ -245,61 +248,105 @@
     )
     couple_real = as_column(couple_rows[0:1])
     couple_imag = as_column(couple_rows[1:2])
-    own_first = as_column(owner_rows) == which_side
+    own_first_column = as_column(owner_rows)
 
     for piece in range(pieces - lag, pieces):
         forward(piece)
 
-    def combine(piece):
-        sibling_copy(piece, 0).wait_recv()
-        sibling_copy(piece, 1).wait_recv()
-        here = prepared[piece].astype(F32)
-        there = theirs[piece].astype(F32)
+    scratch_rows = [couple_real_cols, couple_imag_cols, owner_cols]
+    for place, column in zip(scratch_rows, (couple_real, couple_imag, own_first_column)):
+        place[...] = column
+
+    def combine(piece, rows):
+        here = prepared[piece, rows, :].astype(F32)
+        there = theirs[piece, rows, :].astype(F32)
+        own_first = owner_cols[rows, :] == which_side
         first_part = jnp.where(own_first, here, there)
         other_part = jnp.where(own_first, there, here)
         return (
-            first_part + couple_real * other_part + couple_imag * turned(other_part, piece)
+            first_part
+            + couple_real_cols[rows, :] * other_part
+            + couple_imag_cols[rows, :] * turned(other_part, piece)
         ).astype(BF16)
 
-    def rows_of(level, piece, rows, field):
-        real_part = dot(weights[level, 0, rows, :], field)
-        imag_part = dot(weights[level, 1, rows, :], field)
-        return (real_part + turned(imag_part, piece)).astype(BF16)
+    def products(level, rows, cols, field):
+        return (
+            dot(weights[level, 0, rows, cols], field),
+            dot(weights[level, 1, rows, cols], field),
+        )
+
+    def rounded(parts, piece):
+        return (parts[0] + turned(parts[1], piece)).astype(BF16)
 
     loaded = set()
+    done = set()
+
+    def finish(tile):
+        low_piece, high_piece = sources_of(tile)
+        out_ref[:, tile * LANES : (tile + 1) * LANES] = jnp.where(
+            low_lanes, final[low_piece].astype(F32), final[high_piece].astype(F32)
+        ).astype(BF16)
+
+    def sources_of(tile):
+        return [
+            place if place < pieces else place - pieces for place in (2 * tile, 2 * tile + 1)
+        ]
 
     def run_level(level, piece):
-        if level == 0:
-            field = combine(piece)
-        else:
-            level_copy(level, piece).wait_recv()
-            field = inputs[level, piece]
+        kept_here, other_here = rows_at(bits[level]), rows_at(1 - bits[level])
         if level not in loaded:
             loads[5 + level].wait()
             loaded.add(level)
         if level + 1 < levels:
             bit = bits[level + 1]
-            outgoing[level, piece] = rows_of(level, piece, rows_at(1 - bit), field)
-            level_copy(level + 1, piece).start()
-            inputs[level + 1, piece, rows_at(bit), :] = rows_of(
-                level, piece, rows_at(bit), field
-            )
+            order = [rows_at(1 - bit), rows_at(bit)]
         else:
-            final[piece] = rows_of(level, piece, slice(None), field)
-
-    for step in range(pieces + levels - 1):
+            order = [slice(0, half), slice(half, height)]
+        if level == 0:
+            sibling_copy(piece, 0).wait_recv()
+            own_field = combine(piece, kept_here)
+        else:
+            own_field = inputs[level, piece, kept_here, :]
+        early = piece in early_pieces
+        if early:
+            own_parts = [products(level, rows, kept_here, own_field) for rows in order]
+        if level == 0:
+            sibling_copy(piece, 1).wait_recv()
+            partner_field = combine(piece, other_here)
+        else:
+            level_copy(level, piece).wait_recv()
+            partner_field = inputs[level, piece, other_here, :]
+        if not early:
+            if level == 0:
+                inputs[0, piece, kept_here, :] = own_field
+                inputs[0, piece, other_here, :] = partner_field
+            field = inputs[level, piece]
+        for place, rows in enumerate(order):
+            if early:
+                partner_parts = products(level, rows, other_here, partner_field)
+                parts = [a + b for a, b in zip(own_parts[place], partner_parts)]
+            else:
+                parts = products(level, rows, slice(None), field)
+            value = rounded(parts, piece)
+            if level + 1 == levels:
+                final[piece, rows, :] = value
+            elif place == 0:
+                outgoing[level, piece] = value
+                level_copy(level + 1, piece).start()
+            else:
+                inputs[level + 1, piece, rows, :] = value
+        if level + 1 == levels:
+            done.add(piece)
+            for tile in range(pieces):
+                if piece in sources_of(tile) and done.issuperset(sources_of(tile)):
+                    finish(tile)
+
+    early_pieces = {pieces - 1}
+    for step in range(pieces + 2 * levels):
         for level in range(levels):
-            piece = step - level
+            piece = step - (level + (level > 0))
             if 0 <= piece < pieces:
                 run_level(level, piece)
-
-    for tile in range(pieces):
-        low_piece, high_piece = [
-            place if place < pieces else place - pieces for place in (2 * tile, 2 * tile + 1)
-        ]
-        out_ref[:, tile * LANES : (tile + 1) * LANES] = jnp.where(
-            low_lanes, final[low_piece].astype(F32), final[high_piece].astype(F32)
-        ).astype(BF16)
 
     for copy in small:
         copy.wait_send()
@@ -342,6 +389,9 @@
             pltpu.VMEM((pieces, height, LANES), BF16),
             pltpu.VMEM(coupling.shape, coupling.dtype),
             pltpu.VMEM(owner_map.shape, owner_map.dtype),
+            pltpu.VMEM((height, LANES), coupling.dtype),
+            pltpu.VMEM((height, LANES), coupling.dtype),
+            pltpu.VMEM((height, LANES), owner_map.dtype),
             dma((5 + levels,)),
             dma((2,)),
             dma((2,)),

time: 30.3 us -> 28.8 us (0.950)
  Pallas kernels: 29.3 us -> 27.8 us
    pallas_call x1, Pallas kernels: 29.3 us -> 27.8 us  [body(): pl.pallas_call(functools.partial(kernel, levels), out_shape=jax.ShapeDtyp...]
where the time goes in v3:
time: 28.8 us; the launch traced here: 28.6 us
  Pallas kernels  27.8 us (97%)
  local copies, waits for them, and re-layouts  0.84 us (3%)
    pallas_call x1, Pallas kernels, body(): pl.pallas_call(functools.partial(kernel, levels), out_shape=jax.ShapeDtyp...  27.8 us
    unnamed x1, local copies, waits for them, and re-layouts  0.84 us

profile of v3, /device:TPU:0, one launch (start us, length us, event | category | flops | bytes accessed | tf_op | source)
XLA Modules:
  0.0 28.6 jit_solution(16105763711687884892)
XLA Ops:
  0.0 27.8 %apply.1 = bf16[512,640]{1,0:T(8,128)(2,1)S(1)} custom-call(s32[1,512]{1,0:T(1,128)} %perm_hbm.1, s32[2,512]{1,0:T(2,128)} %owner_hbm.1, f32[2,512]{1,0:T(2,128)} %couple_hbm.1, bf16[512,640]{1,0:T(8,128)(2,1)} %source_hbm.1, bf16[512,512]{1,0:T(8,128)(2,1)} %factor_hbm.1, bf16[3,2,512,512]{3,2,1,0:T(8,128)(2,1)} %transfer_hbm.1), custom_call_target="tpu_custom_call" | custom-call | tf_op jit(solution)/shard_map/apply/pallas_call | solution.py:370
  27.8 0.8 %copy.8 = bf16[512,640]{1,0:T(8,128)(2,1)} copy(bf16[512,640]{1,0:T(8,128)(2,1)S(1)} %apply.1) | data formatting | bytes 1310720
